TPU v7x, 32 devices: a whole 2x2x4 slice. The times are simulated.
32 devices in a mesh: row: 4 (over y, core), blk: 8 (over z, x).
Axes of the slice: x: 2, y: 2, z: 4, core: 2. Of those that a mesh axis runs over, the one named last changes fastest.
Arguments:
- right_side: float32 [4, 8, 8, 32, 256], P('row', 'blk')
- noise_level: float32 [4, 8, 8, 256], P('row', 'blk'), may hold values from 3 to 6
- near_blocks: bfloat16 [4, 8, 8, 9, 256, 256], P('row', 'blk'), as said below
- skeleton_basis: bfloat16 [4, 8, 8, 64, 256], P('row', 'blk'), may hold values from -0.125 to 0.125
- skeleton_index: int32 [4, 8, 64], P('row', 'blk'), may hold values from 0 to 2047, as said below
- far_list: int32 [4, 8, 7], P('row', 'blk'), may hold values from 0 to 7, as said below
- couplings: bfloat16 [4, 8, 7, 64, 64], P('row', 'blk'), as said below
Outputs:
- solution: float32 [4, 8, 8, 32, 256], P('row', 'blk')
- residual: float32 [4, 8, 8, 32, 256], P('row', 'blk')
- quadratic: float32 [32], replicated
Inputs may be any that keep to these rules, and one draw needn't show every extreme that they name: `far_list`: each device's 7 entries are distinct, none is the device's own blk index, and the two cyclic neighbours along blk are always among them; box b lists box b' exactly when b' lists b, and within a row every box's far boxes lie at the same set of cyclic offsets from its own index. `couplings`: the coupling that box b holds for far box b' is the transpose of the one that b' holds for b. `near_blocks`: A leaf's block for near slot s is the transpose of the block that its slot-s neighbour holds for slot 8 - s; slot 4 blocks are symmetric. `skeleton_index`: each device's 64 entries are distinct tracers of its 2048.
All inputs are finite; a program needn't handle non-finite values.
Results may differ from a plain program's by a relative error of at most 0.03.
Values may be sent and summed in bfloat16 or wider, within the bound.
A program may use at most 64 MiB of HBM per device.

v0:
```python
import jax
import jax.numpy as jnp
from jax import lax
from jax.sharding import PartitionSpec as P

ITERS = 4
LEAF_ROWS = 2
LEAF_COLS = 4


def extended_2(array, sides, width):
    for axis, dim in sides:
        count, length = (lax.axis_size(axis), array.shape[dim])
        up = [(i, (i + 1) % count) for i in range(count)]
        down = [(j, i) for i, j in up]
        last = lax.slice_in_dim(array, length - width, length, axis=dim)
        leading = lax.slice_in_dim(array, 0, width, axis=dim)
        before = lax.ppermute(last, axis, up)
        after = lax.ppermute(leading, axis, down)
        array = jnp.concatenate([before, array, after], axis=dim)
    return array


def local(
    right_side, noise_level, near_blocks, skeleton_basis, skeleton_index, far_list, couplings
):
    local_noise = noise_level[0, 0][:, None, :]
    leaf_count = near_blocks.shape[2]
    width = near_blocks.shape[4]
    blocks_grid = near_blocks[0, 0].reshape(LEAF_ROWS, LEAF_COLS, 9, width, width)
    basis_local = skeleton_basis[0, 0]
    skeleton_local = skeleton_index[0, 0]
    far_local = far_list[0, 0]
    coupling_local = couplings[0, 0]
    points = basis_local.shape[2]
    owner_leaf = skeleton_local // points
    owner_point = skeleton_local % points

    def column_sum(values):
        return jnp.sum(values, axis=(0, 1, 2, 4))

    def residual_sum(values):
        return lax.psum(column_sum(values * values), ("row", "blk"))

    solution = jnp.zeros_like(right_side)
    residual = right_side
    direction = right_side
    norm_now = residual_sum(residual)
    for step_index in range(ITERS):
        rounded = direction.astype(jnp.bfloat16)
        own_field = rounded[0, 0]
        columns = own_field.shape[1]
        leaf_grid = own_field.reshape(LEAF_ROWS, LEAF_COLS, columns, width)
        extended = extended_2(leaf_grid, (("row", 0), ("blk", 1)), 1)
        sources = jnp.stack(
            [
                extended[slot // 3 : slot // 3 + LEAF_ROWS, slot % 3 : slot % 3 + LEAF_COLS]
                for slot in range(9)
            ],
            axis=2,
        )
        near = jnp.einsum(
            "abkci,abkij->abcj", sources, blocks_grid, preferred_element_type=jnp.float32
        )
        result = near.reshape(leaf_count, columns, width)
        picked = own_field[owner_leaf, :, owner_point].astype(jnp.float32)
        skeleton = picked.T + jnp.einsum(
            "lci,lki->ck", own_field, basis_local, preferred_element_type=jnp.float32
        )
        all_skeletons = lax.all_gather(
            skeleton.astype(jnp.bfloat16)[None], "blk", axis=0, tiled=True
        )
        selected = all_skeletons[far_local]
        far_sum = jnp.einsum(
            "jck,jkm->cm", selected, coupling_local, preferred_element_type=jnp.float32
        )
        result = result + jnp.einsum(
            "ck,lki->lci",
            far_sum.astype(jnp.bfloat16),
            basis_local,
            preferred_element_type=jnp.float32,
        )
        result = result.at[owner_leaf, :, owner_point].add(far_sum.T)
        applied = (local_noise * direction[0, 0] + result)[None, None]
        curve = lax.psum(column_sum(direction * applied), ("row", "blk"))
        step_size = norm_now / curve
        solution = solution + step_size[:, None] * direction
        residual = residual - step_size[:, None] * applied
        norm_next = residual_sum(residual)
        direction = residual + (norm_next / norm_now)[:, None] * direction
        norm_now = norm_next
    total = lax.psum(column_sum(right_side * solution), ("row", "blk"))
    tracer_count = (
        lax.axis_size("row") * lax.axis_size("blk") * right_side.shape[2] * right_side.shape[4]
    )
    quadratic = total / tracer_count
    return (solution, residual, quadratic)


def solution(mesh):
    return jax.shard_map(
        local,
        mesh=mesh,
        in_specs=(
            P("row", "blk", None, None, None),
            P("row", "blk", None, None),
            P("row", "blk", None, None, None, None),
            P("row", "blk", None, None, None),
            P("row", "blk", None),
            P("row", "blk", None),
            P("row", "blk", None, None, None),
        ),
        out_specs=(P("row", "blk", None, None, None), P("row", "blk", None, None, None), P()),
        check_vma=False,
    )
```

profile of v0, /device:TPU:0, one launch (start us, length us, event | category | flops | bytes accessed | tf_op | source)
XLA Modules:
  0.0 537.6 jit_solution(16591721626279821936)
XLA Ops:
  1.9 2.5 collective-permute-start.1
  5.8 30.8 %all-gather = bf16[256,64]{1,0:T(8,128)(2,1)S(1)} all-gather(bf16[32,64]{1,0:T(8,128)(2,1)S(1)} %fusion.12), channel_id=2, replica_groups=mesh['row'=4,'blk'=8] {'blk'}, dimensions={0}, use_global_device_ids=true | all-gather | bytes 36864 | tf_op jit(solution)/shard_map/all_gather | solution.py:70
  37.3 4.2 collective-permute-start.3
  43.5 5.1 collective-permute-done.2
  48.8 5.4 %fusion.95 = f32[2,4,32,256,1]{3,2,4,1,0:T(8,128)S(1)} fusion(bf16[2,4,9,32,256]{4,3,2,1,0:T(8,128)(2,1)S(1)} %fusion.58, bf16[2,4,9,256,256]{4,3,2,1,0:T(8,128)(2,1)} %bitcast.461), kind=kOutput, calls=%fused_computation.214 | convolution fusion | flops 301989888 | bytes 10878976 | tf_op jit(solution)/shard_map/abkci,abkij->abcj/dot_general | solution.py:62
  54.7 3.7 scatter_fusion
  59.0 36.9 %all-reduce = (f32[32]{0:T(128)S(1)}, f32[32]{0:T(128)S(1)}) all-reduce(f32[32]{0:T(128)S(1)} %get-tuple-element.32, f32[32]{0:T(128)S(1)} %fusion.16), channel_id=1, replica_groups=mesh['row'=4,'blk'=8] {'row','blk'}, use_global_device_ids=true, to_apply=%region_1.2 | all-reduce | flops 64 | bytes 512 | tf_op jit(solution)/shard_map/psum | solution.py:43
  96.1 42.0 %psum.65 = f32[32]{0:T(128)S(1)} all-reduce(f32[32]{0:T(128)S(1)} %multiply_reduce_fusion.3), channel_id=1, replica_groups=mesh['row'=4,'blk'=8] {'row','blk'}, use_global_device_ids=true, to_apply=%region_6.7 | all-reduce | flops 32 | bytes 256 | tf_op jit(solution)/shard_map/psum | solution.py:43
  140.2 30.6 %all-gather.1 = bf16[256,64]{1,0:T(8,128)(2,1)S(1)} all-gather(bf16[32,64]{1,0:T(8,128)(2,1)S(1)} %fusion.13), channel_id=3, replica_groups=mesh['row'=4,'blk'=8] {'blk'}, dimensions={0}, use_global_device_ids=true | all-gather | bytes 36864 | tf_op jit(solution)/shard_map/all_gather | solution.py:70
  171.4 3.2 collective-permute-start.7
  174.9 1.6 collective-permute-done.7
  176.5 5.1 collective-permute-done.6
  181.8 5.4 %fusion.96 = f32[2,4,32,256,1]{3,2,4,1,0:T(8,128)S(1)} fusion(bf16[2,4,9,32,256]{4,3,2,1,0:T(8,128)(2,1)S(1)} %fusion.48, bf16[2,4,9,256,256]{4,3,2,1,0:T(8,128)(2,1)} %bitcast.462), kind=kOutput, calls=%fused_computation.215 | convolution fusion | flops 301989888 | bytes 10878976 | tf_op jit(solution)/shard_map/abkci,abkij->abcj/dot_general | solution.py:62
  187.7 3.7 scatter_fusion.1
  191.9 36.9 %psum.66 = f32[32]{0:T(128)S(1)} all-reduce(f32[32]{0:T(128)S(1)} %fusion.19), channel_id=1, replica_groups=mesh['row'=4,'blk'=8] {'row','blk'}, use_global_device_ids=true, to_apply=%region_9.10 | all-reduce | flops 32 | bytes 256 | tf_op jit(solution)/shard_map/psum | solution.py:85
  229.0 41.7 %psum.67 = f32[32]{0:T(128)S(1)} all-reduce(f32[32]{0:T(128)S(1)} %get-tuple-element.13), channel_id=1, replica_groups=mesh['row'=4,'blk'=8] {'row','blk'}, use_global_device_ids=true, to_apply=%region_11.12 | all-reduce | flops 32 | bytes 256 | tf_op jit(solution)/shard_map/psum | solution.py:43
  272.9 30.5 %all-gather.2 = bf16[256,64]{1,0:T(8,128)(2,1)S(1)} all-gather(bf16[32,64]{1,0:T(8,128)(2,1)S(1)} %fusion.14), channel_id=4, replica_groups=mesh['row'=4,'blk'=8] {'blk'}, dimensions={0}, use_global_device_ids=true | all-gather | bytes 36864 | tf_op jit(solution)/shard_map/all_gather | solution.py:70
  304.1 3.2 collective-permute-start.11
  307.5 1.6 collective-permute-done.11
  309.2 5.1 collective-permute-done.10
  314.5 5.4 %fusion.97 = f32[2,4,32,256,1]{3,2,4,1,0:T(8,128)S(1)} fusion(bf16[2,4,9,32,256]{4,3,2,1,0:T(8,128)(2,1)S(1)} %fusion.38, bf16[2,4,9,256,256]{4,3,2,1,0:T(8,128)(2,1)} %bitcast.463), kind=kOutput, calls=%fused_computation.216 | convolution fusion | flops 301989888 | bytes 10878976 | tf_op jit(solution)/shard_map/abkci,abkij->abcj/dot_general | solution.py:62
  320.4 3.7 scatter_fusion.2
  324.5 36.9 %psum.68 = f32[32]{0:T(128)S(1)} all-reduce(f32[32]{0:T(128)S(1)} %fusion.18), channel_id=1, replica_groups=mesh['row'=4,'blk'=8] {'row','blk'}, use_global_device_ids=true, to_apply=%region_14.15 | all-reduce | flops 32 | bytes 256 | tf_op jit(solution)/shard_map/psum | solution.py:85
  361.6 42.0 %psum.69 = f32[32]{0:T(128)S(1)} all-reduce(f32[32]{0:T(128)S(1)} %get-tuple-element.9), channel_id=1, replica_groups=mesh['row'=4,'blk'=8] {'row','blk'}, use_global_device_ids=true, to_apply=%region_16.17 | all-reduce | flops 32 | bytes 256 | tf_op jit(solution)/shard_map/psum | solution.py:43
  405.7 30.6 %all-gather.3 = bf16[256,64]{1,0:T(8,128)(2,1)S(1)} all-gather(bf16[32,64]{1,0:T(8,128)(2,1)S(1)} %fusion.15), channel_id=5, replica_groups=mesh['row'=4,'blk'=8] {'blk'}, dimensions={0}, use_global_device_ids=true | all-gather | bytes 36864 | tf_op jit(solution)/shard_map/all_gather | solution.py:70
  436.9 3.2 collective-permute-start.15
  440.4 1.6 collective-permute-done.15
  442.1 5.1 collective-permute-done.14
  447.4 5.4 %fusion.98 = f32[2,4,32,256,1]{3,2,4,1,0:T(8,128)S(1)} fusion(bf16[2,4,9,32,256]{4,3,2,1,0:T(8,128)(2,1)S(1)} %fusion.28, bf16[2,4,9,256,256]{4,3,2,1,0:T(8,128)(2,1)} %bitcast.464), kind=kOutput, calls=%fused_computation.217 | convolution fusion | flops 301989888 | bytes 10878976 | tf_op jit(solution)/shard_map/abkci,abkij->abcj/dot_general | solution.py:62
  453.3 3.7 scatter_fusion.3
  457.4 36.9 %psum.70 = f32[32]{0:T(128)S(1)} all-reduce(f32[32]{0:T(128)S(1)} %fusion.17), channel_id=1, replica_groups=mesh['row'=4,'blk'=8] {'row','blk'}, use_global_device_ids=true, to_apply=%region_19.20 | all-reduce | flops 32 | bytes 256 | tf_op jit(solution)/shard_map/psum | solution.py:85
  495.4 41.7 %psum.71 = f32[32]{0:T(128)S(1)} all-reduce(f32[32]{0:T(128)S(1)} %get-tuple-element.5), channel_id=1, replica_groups=mesh['row'=4,'blk'=8] {'row','blk'}, use_global_device_ids=true, to_apply=%region_21.22 | all-reduce | flops 32 | bytes 256 | tf_op jit(solution)/shard_map/psum | solution.py:92
  (145 shorter events, 20.9 us)
Async XLA Ops:
  0.6 5.0 copy-start
  0.6 4.0 copy-start.4
  0.7 36.0 %copy-start.5 = (s32[1,1,7]{2,1,0:T(1,128)S(1)}, s32[1,1,7]{2,1,0:T(1,128)}, u32[]{:S(2)}) copy-start(s32[1,1,7]{2,1,0:T(1,128)} %param.12) | copy-start | bytes 88
  0.7 40.9 %copy-start.2 = (bf16[1,1,7,64,64]{4,3,2,1,0:T(8,128)(2,1)S(1)}, bf16[1,1,7,64,64]{4,3,2,1,0:T(8,128)(2,1)}, u32[]{:S(2)}) copy-start(bf16[1,1,7,64,64]{4,3,2,1,0:T(8,128)(2,1)} %param.13) | copy-start | bytes 172036
  1.9 39.9 %copy-start.1 = (f32[1,1,8,32,256]{4,3,2,1,0:T(8,128)S(1)}, f32[1,1,8,32,256]{4,3,2,1,0:T(8,128)}, u32[]{:S(2)}) copy-start(f32[1,1,8,32,256]{4,3,2,1,0:T(8,128)} %param.7) | copy-start | bytes 786436
  1.9 35.3 %collective-permute-start.1 = (bf16[1,4,32,256]{3,2,1,0:T(8,128)(2,1)S(1)}, bf16[1,4,32,256]{3,2,1,0:T(8,128)(2,1)S(1)}, u32[]{:S(2)}, u32[]{:S(2)}) collective-permute-start(bf16[1,4,32,256]{3,2,1,0:T(8,128)(2,1)S(1)} %get-tuple-element.45), channel_id=1, source_target_pairs={{8,0},{16,8},{24,16},{0,24},{9,1},{17,9},{25,17},{1,25},{10,2},{18... | collective-permute-start | bytes 196616 | tf_op jit(solution)/shard_map/ppermute | solution.py:19
  4.4 32.9 %collective-permute-start = (bf16[1,4,32,256]{3,2,1,0:T(8,128)(2,1)S(1)}, bf16[1,4,32,256]{3,2,1,0:T(8,128)(2,1)S(1)}, u32[]{:S(2)}, u32[]{:S(2)}) collective-permute-start(bf16[1,4,32,256]{3,2,1,0:T(8,128)(2,1)S(1)} %get-tuple-element.44), channel_id=1, source_target_pairs={{0,8},{8,16},{16,24},{24,0},{1,9},{9,17},{17,25},{25,1},{2,10},{10... | collective-permute-start | bytes 196616 | tf_op jit(solution)/shard_map/ppermute | solution.py:18
  37.3 6.1 %collective-permute-start.3 = (bf16[4,1,32,256]{3,2,1,0:T(8,128)(2,1)S(1)}, bf16[4,1,32,256]{3,2,1,0:T(8,128)(2,1)S(1)}, u32[]{:S(2)}, u32[]{:S(2)}) collective-permute-start(bf16[4,1,32,256]{3,2,1,0:T(8,128)(2,1)S(1)} %get-tuple-element.36), channel_id=1, source_target_pairs={{1,0},{2,1},{3,2},{4,3},{5,4},{6,5},{7,6},{0,7},{9,8},{10,9},{11,1... | collective-permute-start | bytes 196616 | tf_op jit(solution)/shard_map/ppermute | solution.py:19
  41.5 7.0 %collective-permute-start.2 = (bf16[4,1,32,256]{3,2,1,0:T(8,128)(2,1)S(1)}, bf16[4,1,32,256]{3,2,1,0:T(8,128)(2,1)S(1)}, u32[]{:S(2)}, u32[]{:S(2)}) collective-permute-start(bf16[4,1,32,256]{3,2,1,0:T(8,128)(2,1)S(1)} %get-tuple-element.37), channel_id=1, source_target_pairs={{0,1},{1,2},{2,3},{3,4},{4,5},{5,6},{6,7},{7,0},{8,9},{9,10},{10,1... | collective-permute-start | bytes 196616 | tf_op jit(solution)/shard_map/ppermute | solution.py:18
  48.7 5.4 %copy-start.3 = (f32[1,1,8,256]{3,2,1,0:T(8,128)S(1)}, f32[1,1,8,256]{3,2,1,0:T(8,128)}, u32[]{:S(2)}) copy-start(f32[1,1,8,256]{3,2,1,0:T(8,128)} %param.8) | copy-start | bytes 24580
  138.2 33.1 %collective-permute-start.5 = (bf16[1,4,32,256]{3,2,1,0:T(8,128)(2,1)S(1)}, bf16[1,4,32,256]{3,2,1,0:T(8,128)(2,1)S(1)}, u32[]{:S(2)}, u32[]{:S(2)}) collective-permute-start(bf16[1,4,32,256]{3,2,1,0:T(8,128)(2,1)S(1)} %get-tuple-element.43), channel_id=1, source_target_pairs={{8,0},{16,8},{24,16},{0,24},{9,1},{17,9},{25,17},{1,25},{10,2},{18... | collective-permute-start | bytes 196616 | tf_op jit(solution)/shard_map/ppermute | solution.py:19
  138.6 32.7 %collective-permute-start.4 = (bf16[1,4,32,256]{3,2,1,0:T(8,128)(2,1)S(1)}, bf16[1,4,32,256]{3,2,1,0:T(8,128)(2,1)S(1)}, u32[]{:S(2)}, u32[]{:S(2)}) collective-permute-start(bf16[1,4,32,256]{3,2,1,0:T(8,128)(2,1)S(1)} %get-tuple-element.42), channel_id=1, source_target_pairs={{0,8},{8,16},{16,24},{24,0},{1,9},{9,17},{17,25},{25,1},{2,10},{10... | collective-permute-start | bytes 196616 | tf_op jit(solution)/shard_map/ppermute | solution.py:18
  171.4 5.2 collective-permute-start.7
  174.6 7.0 %collective-permute-start.6 = (bf16[4,1,32,256]{3,2,1,0:T(8,128)(2,1)S(1)}, bf16[4,1,32,256]{3,2,1,0:T(8,128)(2,1)S(1)}, u32[]{:S(2)}, u32[]{:S(2)}) collective-permute-start(bf16[4,1,32,256]{3,2,1,0:T(8,128)(2,1)S(1)} %get-tuple-element.31), channel_id=1, source_target_pairs={{0,1},{1,2},{2,3},{3,4},{4,5},{5,6},{6,7},{7,0},{8,9},{9,10},{10,1... | collective-permute-start | bytes 196616 | tf_op jit(solution)/shard_map/ppermute | solution.py:18
  270.9 33.2 %collective-permute-start.9 = (bf16[1,4,32,256]{3,2,1,0:T(8,128)(2,1)S(1)}, bf16[1,4,32,256]{3,2,1,0:T(8,128)(2,1)S(1)}, u32[]{:S(2)}, u32[]{:S(2)}) collective-permute-start(bf16[1,4,32,256]{3,2,1,0:T(8,128)(2,1)S(1)} %get-tuple-element.41), channel_id=1, source_target_pairs={{8,0},{16,8},{24,16},{0,24},{9,1},{17,9},{25,17},{1,25},{10,2},{18... | collective-permute-start | bytes 196616 | tf_op jit(solution)/shard_map/ppermute | solution.py:19
  271.5 32.5 %collective-permute-start.8 = (bf16[1,4,32,256]{3,2,1,0:T(8,128)(2,1)S(1)}, bf16[1,4,32,256]{3,2,1,0:T(8,128)(2,1)S(1)}, u32[]{:S(2)}, u32[]{:S(2)}) collective-permute-start(bf16[1,4,32,256]{3,2,1,0:T(8,128)(2,1)S(1)} %get-tuple-element.40), channel_id=1, source_target_pairs={{0,8},{8,16},{16,24},{24,0},{1,9},{9,17},{17,25},{25,1},{2,10},{10... | collective-permute-start | bytes 196616 | tf_op jit(solution)/shard_map/ppermute | solution.py:18
  304.1 5.1 collective-permute-start.11
  307.3 7.0 %collective-permute-start.10 = (bf16[4,1,32,256]{3,2,1,0:T(8,128)(2,1)S(1)}, bf16[4,1,32,256]{3,2,1,0:T(8,128)(2,1)S(1)}, u32[]{:S(2)}, u32[]{:S(2)}) collective-permute-start(bf16[4,1,32,256]{3,2,1,0:T(8,128)(2,1)S(1)} %get-tuple-element.27), channel_id=1, source_target_pairs={{0,1},{1,2},{2,3},{3,4},{4,5},{5,6},{6,7},{7,0},{8,9},{9,10},{10,1... | collective-permute-start | bytes 196616 | tf_op jit(solution)/shard_map/ppermute | solution.py:18
  403.8 33.1 %collective-permute-start.13 = (bf16[1,4,32,256]{3,2,1,0:T(8,128)(2,1)S(1)}, bf16[1,4,32,256]{3,2,1,0:T(8,128)(2,1)S(1)}, u32[]{:S(2)}, u32[]{:S(2)}) collective-permute-start(bf16[1,4,32,256]{3,2,1,0:T(8,128)(2,1)S(1)} %get-tuple-element.39), channel_id=1, source_target_pairs={{8,0},{16,8},{24,16},{0,24},{9,1},{17,9},{25,17},{1,25},{10,2},{18... | collective-permute-start | bytes 196616 | tf_op jit(solution)/shard_map/ppermute | solution.py:19
  404.1 32.7 %collective-permute-start.12 = (bf16[1,4,32,256]{3,2,1,0:T(8,128)(2,1)S(1)}, bf16[1,4,32,256]{3,2,1,0:T(8,128)(2,1)S(1)}, u32[]{:S(2)}, u32[]{:S(2)}) collective-permute-start(bf16[1,4,32,256]{3,2,1,0:T(8,128)(2,1)S(1)} %get-tuple-element.38), channel_id=1, source_target_pairs={{0,8},{8,16},{16,24},{24,0},{1,9},{9,17},{17,25},{25,1},{2,10},{10... | collective-permute-start | bytes 196616 | tf_op jit(solution)/shard_map/ppermute | solution.py:18
  436.9 5.2 collective-permute-start.15
  440.2 7.0 %collective-permute-start.14 = (bf16[4,1,32,256]{3,2,1,0:T(8,128)(2,1)S(1)}, bf16[4,1,32,256]{3,2,1,0:T(8,128)(2,1)S(1)}, u32[]{:S(2)}, u32[]{:S(2)}) collective-permute-start(bf16[4,1,32,256]{3,2,1,0:T(8,128)(2,1)S(1)} %get-tuple-element.23), channel_id=1, source_target_pairs={{0,1},{1,2},{2,3},{3,4},{4,5},{5,6},{6,7},{7,0},{8,9},{9,10},{10,1... | collective-permute-start | bytes 196616 | tf_op jit(solution)/shard_map/ppermute | solution.py:18
where the time goes:
time: 539 us; the launch traced here: 538 us
  blocking collectives  438 us (81%)
  waiting for transfers between devices  26.4 us (5%)
  matrix products  23.9 us (4%)
  other arithmetic  19.6 us (4%)
  starting transfers between devices  18.2 us (3%)
  local copies, waits for them, and re-layouts  10.6 us (2%)
    psum x4, blocking collectives, residual_sum(): return lax.psum(column_sum(values * values), ('row', 'blk'))  163 us
    all_gather x4, blocking collectives, local(): lax.all_gather(skeleton.astype(jnp.bfloat16)[None], 'blk', axis=0, tiled=...  123 us
    psum x3, blocking collectives, local(): curve = lax.psum(column_sum(direction * applied), ('row', 'blk'))  111 us
    psum x1, blocking collectives, local(): total = lax.psum(column_sum(right_side * solution), ('row', 'blk'))  41.7 us
    dot_general x4, matrix products, local(): jnp.einsum('abkci,abkij->abcj', sources, blocks_grid, preferred_element_t...  21.6 us
    ppermute x8, waiting for transfers between devices, extended_2(): before = lax.ppermute(last, axis, up)  20.2 us
    ppermute x8, starting transfers between devices, extended_2(): after = lax.ppermute(leading, axis, down)  17.8 us
    scatter-add x4, other arithmetic, local(): result = result.at[owner_leaf, :, owner_point].add(far_sum.T)  14.7 us
  transfers between devices with their start and end apart: 16, of which 8 were waited for; matrix products, arithmetic and copies ran while one was open for 2% of the time, Pallas kernels for 0%

commit v1 on v0

v1 whole, which is shorter than its diff:
```python
import functools

import jax
import jax.numpy as jnp
from jax import lax
from jax.experimental import pallas as pl
from jax.experimental.pallas import tpu as pltpu
from jax.sharding import PartitionSpec as P

ITERS = 4
LEAF_ROWS = 2
LEAF_COLS = 4
MESH = pl.DeviceIdType.MESH
HIGHEST = lax.Precision.HIGHEST
SHIFTS = ((-1, 0), (1, 0), (0, -1), (0, 1), (-1, -1), (-1, 1), (1, -1), (1, 1))


def span(shift, count, incoming):
    if shift == 0:
        return 1, count
    if incoming:
        return (0 if shift > 0 else count + 1), 1
    return (count if shift > 0 else 1), 1


def each(count, body):
    if count <= 16:
        for i in range(count):
            body(i)
    else:
        pl.loop(0, count)(body)


def kernel(
    n_row, n_blk, tracers,
    right_ref, noise_ref, blocks_hbm, basis_ref, index_ref, far_ref, coupling_ref,
    solution_ref, residual_ref, quadratic_ref,
    blocks, mixed, extended, direction, applied, skeletons, row_sums, blk_sums,
    load_sem, halo_send, halo_recv, skel_send, skel_recv, row_send, row_recv, blk_send, blk_recv,
):
    leaves, columns, width = right_ref.shape
    rank = basis_ref.shape[1]
    far_count = coupling_ref.shape[0]
    my_row, my_blk = lax.axis_index("row"), lax.axis_index("blk")

    loads = [
        pltpu.make_async_copy(blocks_hbm.at[l], blocks.at[l], load_sem.at[l]) for l in range(leaves)
    ]
    for load in loads:
        load.start()

    def row_at(o):
        return lax.rem(my_row + (o + n_row), n_row)

    def blk_at(o):
        return lax.rem(my_blk + (o + n_blk), n_blk)

    barrier = pltpu.get_barrier_semaphore()

    def greet(row, blk):
        pl.semaphore_signal(barrier, inc=1, device_id={"row": row, "blk": blk}, device_id_type=MESH)

    for o in range(1, n_row):
        greet(row_at(o), my_blk)
    each(n_blk - 1, lambda i: greet(my_row, blk_at(i + 1)))
    for dr, dc in SHIFTS[4:]:
        greet(row_at(dr), blk_at(dc))

    sublane = lax.broadcasted_iota(jnp.int32, (rank, rank), 0)
    lane = lax.broadcasted_iota(jnp.int32, (rank, rank), 1)
    as_row = jnp.broadcast_to(index_ref[...].astype(jnp.float32), (rank, rank))
    as_column = jnp.sum(jnp.where(sublane == lane, as_row, 0.0), axis=1, keepdims=True)
    point = lax.broadcasted_iota(jnp.int32, (rank, width), 1).astype(jnp.float32)
    for l in range(leaves):
        picks = jnp.where(point + float(width * l) == as_column, 1.0, 0.0).astype(jnp.bfloat16)
        mixed[l, :rank] = basis_ref[l]
        mixed[l, rank : 2 * rank] = picks
        mixed[l, 2 * rank :] = picks
        value = right_ref[l]
        direction[l] = value
        residual_ref[l] = value
        solution_ref[l] = jnp.zeros_like(value)
    quadratic_ref[...] = jnp.zeros_like(quadratic_ref)

    pl.semaphore_wait(barrier, (n_row - 1) + (n_blk - 1) + 4)

    ones = jnp.ones((8, 128), jnp.float32)
    head = lax.broadcasted_iota(jnp.int32, (8, columns), 0)
    spread_row = lax.broadcasted_iota(jnp.int32, (columns, 128), 0)
    spread_lane = lax.broadcasted_iota(jnp.int32, (columns, 128), 1)

    def halo(k, n):
        dr, dc = SHIFTS[n]
        (sr, nr), (sc, nc) = span(dr, LEAF_ROWS, False), span(dc, LEAF_COLS, False)
        (tr, _), (tc, _) = span(dr, LEAF_ROWS, True), span(dc, LEAF_COLS, True)
        return pltpu.make_async_remote_copy(
            src_ref=extended.at[k, pl.ds(sr, nr), pl.ds(sc, nc)],
            dst_ref=extended.at[k, pl.ds(tr, nr), pl.ds(tc, nc)],
            send_sem=halo_send.at[k, n],
            recv_sem=halo_recv.at[k, n],
            device_id={"row": row_at(dr), "blk": blk_at(dc)},
            device_id_type=MESH,
        )

    def row_copy(k, o):
        return pltpu.make_async_remote_copy(
            src_ref=row_sums.at[k, my_row],
            dst_ref=row_sums.at[k, my_row],
            send_sem=row_send.at[k, o - 1],
            recv_sem=row_recv.at[k, o - 1],
            device_id={"row": row_at(o), "blk": my_blk},
            device_id_type=MESH,
        )

    def blk_copy(buffer, send, recv, k, o):
        return pltpu.make_async_remote_copy(
            src_ref=buffer.at[k, my_blk],
            dst_ref=buffer.at[k, my_blk],
            send_sem=send.at[k],
            recv_sem=recv.at[k],
            device_id={"row": my_row, "blk": blk_at(o)},
            device_id_type=MESH,
        )

    def blk_wait(buffer, sem, k):
        every = buffer.at[k, pl.ds(0, n_blk - 1)]
        pltpu.make_async_copy(every, every, sem.at[k]).wait()

    def slots(l):
        a, c = divmod(l, LEAF_COLS)
        for s in range(9):
            yield s, a + s // 3, c + s % 3

    def inside(row, col):
        return 1 <= row <= LEAF_ROWS and 1 <= col <= LEAF_COLS

    def iteration(k, first):
        for l in range(leaves):
            a, c = divmod(l, LEAF_COLS)
            extended[k, a + 1, c + 1] = direction[l].astype(jnp.bfloat16)
        for n in range(8):
            halo(k, n).start()

        def field(row, col):
            return extended[k, row, col]

        both = jnp.zeros((columns, 2 * rank), jnp.float32)
        for l in range(leaves):
            a, c = divmod(l, LEAF_COLS)
            both = both + lax.dot_general(
                field(a + 1, c + 1), mixed[l, : 2 * rank], (((1,), (1,)), ((), ())),
                preferred_element_type=jnp.float32,
            )
        skeletons[k, my_blk] = (both[:, :rank] + both[:, rank:]).astype(jnp.bfloat16)
        each(n_blk - 1, lambda i: blk_copy(skeletons, skel_send, skel_recv, k, i + 1).start())

        for l in range(leaves):
            if first:
                loads[l].wait()
            total = noise_ref[l : l + 1] * direction[l]
            for s, row, col in slots(l):
                if inside(row, col):
                    total = total + jnp.dot(
                        field(row, col), blocks[l, s], preferred_element_type=jnp.float32
                    )
            applied[l] = total

        blk_wait(skeletons, skel_recv, k)
        far = jnp.zeros((columns, rank), jnp.float32)
        for j in range(far_count):
            far = far + jnp.dot(
                skeletons[k, far_ref[0, j]], coupling_ref[j], preferred_element_type=jnp.float32
            )
        far_high = far.astype(jnp.bfloat16)
        far_low = (far - far_high.astype(jnp.float32)).astype(jnp.bfloat16)
        far_all = jnp.concatenate([far_high, far_high, far_low], axis=1)

        for n in range(8):
            halo(k, n).wait_recv()

        sums = [jnp.zeros((columns, 128), jnp.float32) for _ in range(5)]
        for l in range(leaves):
            total = applied[l] + jnp.dot(far_all, mixed[l], preferred_element_type=jnp.float32)
            for s, row, col in slots(l):
                if not inside(row, col):
                    total = total + jnp.dot(
                        field(row, col), blocks[l, s], preferred_element_type=jnp.float32
                    )
            applied[l] = total
            d, r = direction[l], residual_ref[l]
            for q, product in enumerate((d * total, r * total, total * total, right_ref[l] * d, r * r)):
                for h in range(width // 128):
                    sums[q] = sums[q] + product[:, 128 * h : 128 * (h + 1)]

        part = jnp.zeros((8, columns), jnp.float32)
        for q in range(5):
            line = lax.dot_general(
                ones, sums[q], (((1,), (1,)), ((), ())),
                precision=HIGHEST, preferred_element_type=jnp.float32,
            )
            part = jnp.where(head == q, line, part)
        row_sums[k, my_row] = jnp.concatenate(
            [part, jnp.zeros((8, 128 - columns), jnp.float32)], axis=1
        )
        for o in range(1, n_row):
            row_copy(k, o).start()
        for o in range(1, n_row):
            row_copy(k, o).wait_recv()
        in_row = row_sums[k, 0]
        for i in range(1, n_row):
            in_row = in_row + row_sums[k, i]
        blk_sums[k, my_blk] = in_row
        each(n_blk - 1, lambda i: blk_copy(blk_sums, blk_send, blk_recv, k, i + 1).start())
        blk_wait(blk_sums, blk_recv, k)
        if n_blk <= 16:
            whole = blk_sums[k, 0]
            for i in range(1, n_blk):
                whole = whole + blk_sums[k, i]
        else:
            whole = jnp.sum(blk_sums[k], axis=0)

        curve, cross, square, data, norm = (whole[q : q + 1] for q in range(5))
        step = norm / curve
        norm_next = jnp.maximum(norm - 2.0 * step * cross + step * step * square, 0.0)
        turn = norm_next / norm
        quadratic_ref[...] = quadratic_ref[...] + step * data * (1.0 / tracers)

        def per_column(line):
            wide = jnp.broadcast_to(line, (columns, 128))
            kept = jnp.where(spread_row == spread_lane, wide, 0.0)
            return jnp.sum(kept, axis=1, keepdims=True)

        step_c, turn_c = per_column(step), per_column(turn)
        for l in range(leaves):
            d = direction[l]
            r = residual_ref[l] - step_c * applied[l]
            solution_ref[l] = solution_ref[l] + step_c * d
            residual_ref[l] = r
            direction[l] = r + turn_c * d

        for n in range(8):
            halo(k, n).wait_send()
        for o in range(1, n_row):
            row_copy(k, o).wait_send()
        blk_wait(skeletons, skel_send, k)
        blk_wait(blk_sums, blk_send, k)

    iteration(0, True)

    @pl.loop(1, ITERS)
    def _(k):
        iteration(k, False)


def local(
    n_row, n_blk,
    right_side, noise_level, near_blocks, skeleton_basis, skeleton_index, far_list, couplings,
):
    leaves, columns, width = right_side.shape[2:]
    rank = skeleton_basis.shape[3]
    field = jax.ShapeDtypeStruct((leaves, columns, width), jnp.float32)
    vmem = pl.BlockSpec(memory_space=pltpu.VMEM)
    dma = pltpu.SemaphoreType.DMA
    solution_out, residual_out, quadratic = pl.pallas_call(
        functools.partial(kernel, n_row, n_blk, n_row * n_blk * leaves * width),
        out_shape=(field, field, jax.ShapeDtypeStruct((1, 128), jnp.float32)),
        in_specs=[
            vmem, vmem, pl.BlockSpec(memory_space=pl.ANY), vmem, vmem,
            pl.BlockSpec(memory_space=pltpu.SMEM), vmem,
        ],
        out_specs=(vmem, vmem, vmem),
        scratch_shapes=[
            pltpu.VMEM(near_blocks.shape[2:], jnp.bfloat16),
            pltpu.VMEM((leaves, 3 * rank, width), jnp.bfloat16),
            pltpu.VMEM((ITERS, LEAF_ROWS + 2, LEAF_COLS + 2, columns, width), jnp.bfloat16),
            pltpu.VMEM((leaves, columns, width), jnp.float32),
            pltpu.VMEM((leaves, columns, width), jnp.float32),
            pltpu.VMEM((ITERS, n_blk, columns, rank), jnp.bfloat16),
            pltpu.VMEM((ITERS, n_row, 8, 128), jnp.float32),
            pltpu.VMEM((ITERS, n_blk, 8, 128), jnp.float32),
            dma((leaves,)),
            dma((ITERS, 8)), dma((ITERS, 8)),
            dma((ITERS,)), dma((ITERS,)),
            dma((ITERS, n_row - 1)), dma((ITERS, n_row - 1)),
            dma((ITERS,)), dma((ITERS,)),
        ],
        compiler_params=pltpu.CompilerParams(
            collective_id=0, has_side_effects=True, vmem_limit_bytes=48 * 1024 * 1024
        ),
    )(
        right_side[0, 0], noise_level[0, 0], near_blocks[0, 0], skeleton_basis[0, 0],
        skeleton_index[0], far_list[0], couplings[0, 0],
    )
    return solution_out[None, None], residual_out[None, None], quadratic[0, :columns]


def solution(mesh):
    return jax.shard_map(
        functools.partial(local, mesh.shape["row"], mesh.shape["blk"]),
        mesh=mesh,
        in_specs=(
            P("row", "blk", None, None, None),
            P("row", "blk", None, None),
            P("row", "blk", None, None, None, None),
            P("row", "blk", None, None, None),
            P("row", "blk", None),
            P("row", "blk", None),
            P("row", "blk", None, None, None),
        ),
        out_specs=(P("row", "blk", None, None, None), P("row", "blk", None, None, None), P()),
        check_vma=False,
    )
```

time: 539 us -> 70.9 us (0.13)
  blocking collectives: 438 us -> 0 us
  Pallas kernels: 0 us -> 63.2 us
  waiting for transfers between devices: 26.4 us -> 0 us
  matrix products: 23.9 us -> 0 us
  other arithmetic: 19.6 us -> 0 us
  starting transfers between devices: 18.2 us -> 0 us
    psum x8 -> x0, blocking collectives: 315 us -> none  [the longest x4 163 us: residual_sum(): return lax.psum(column_sum(values * values), ('row', 'blk'))]
    all_gather x4 -> x0, blocking collectives: 123 us -> none  [local(): lax.all_gather(skeleton.astype(jnp.bfloat16)[None], 'blk', axis=0, tiled=...]
    pallas_call x0 -> x1, Pallas kernels: none -> 63.2 us  [local(): pl.pallas_call(functools.partial(kernel, n_row, n_blk, n_row * n_blk * le...]
    ppermute x16 -> x0, waiting for transfers between devices: 26.4 us -> none  [the longest x8 20.2 us: extended_2(): before = lax.ppermute(last, axis, up)]
    dot_general x16 -> x0, matrix products: 23.9 us -> none  [the longest x4 21.6 us: local(): jnp.einsum('abkci,abkij->abcj', sources, blocks_grid, preferred_element_t...]
    ppermute x16 -> x0, starting transfers between devices: 18.2 us -> none  [the longest x8 17.8 us: extended_2(): after = lax.ppermute(leading, axis, down)]
    scatter-add x4 -> x0, other arithmetic: 14.7 us -> none  [local(): result = result.at[owner_leaf, :, owner_point].add(far_sum.T)]
    gather x12 -> x0, local copies, waits for them, and re-layouts: 5.9 us -> none  [the longest x8 3.65 us: local(): picked = own_field[owner_leaf, :, owner_point].astype(jnp.float32)]
  transfers between devices with their start and end apart: 16 -> 0, of which waited for: 8 -> 0; matrix products, arithmetic and copies ran while one was open for 2% -> 0% of each run, Pallas kernels for 0% -> 0%
where the time goes in v1:
time: 70.9 us; the launch traced here: 70.6 us
  Pallas kernels  63.2 us (89%)
  local copies, waits for them, and re-layouts  6.71 us (9%)
    pallas_call x1, Pallas kernels, local(): pl.pallas_call(functools.partial(kernel, n_row, n_blk, n_row * n_blk * le...  63.2 us
    unnamed x14, local copies, waits for them, and re-layouts  6.2 us

profile of v1, /device:TPU:0, one launch (start us, length us, event | category | flops | bytes accessed | tf_op | source)
XLA Modules:
  0.0 70.6 jit_solution(10060881036032177734)
XLA Ops:
  0.6 0.0 copy-start
  0.6 0.9 %copy-done = f32[1,1,8,32,256]{4,3,2,1,0:T(8,128)S(1)} copy-done((f32[1,1,8,32,256]{4,3,2,1,0:T(8,128)S(1)}, f32[1,1,8,32,256]{4,3,2,1,0:T(8,128)}, u32[]{:S(2)}) %copy-start) | copy-done | bytes 262168
  1.6 0.0 copy-start.1
  1.6 0.9 %copy-done.1 = bf16[1,1,8,64,256]{4,3,2,1,0:T(8,128)(2,1)S(1)} copy-done((bf16[1,1,8,64,256]{4,3,2,1,0:T(8,128)(2,1)S(1)}, bf16[1,1,8,64,256]{4,3,2,1,0:T(8,128)(2,1)}, u32[]{:S(2)}) %copy-start.1) | copy-done | bytes 262168
  2.5 0.0 copy-start.2
  2.5 0.9 %copy-done.2 = bf16[1,1,7,64,64]{4,3,2,1,0:T(8,128)(2,1)S(1)} copy-done((bf16[1,1,7,64,64]{4,3,2,1,0:T(8,128)(2,1)S(1)}, bf16[1,1,7,64,64]{4,3,2,1,0:T(8,128)(2,1)}, u32[]{:S(2)}) %copy-start.2) | copy-done | bytes 57368
  3.4 0.0 copy-start.3
  3.4 0.7 copy-done.3
  4.1 0.0 copy-start.4
  4.1 0.7 copy-done.4
  4.8 0.0 copy-start.5
  4.8 0.7 copy-done.5
  5.4 63.2 %shard_map.94 = (f32[8,32,256]{2,1,0:T(8,128)S(1)}, f32[8,32,256]{2,1,0:T(8,128)S(1)}, f32[1,128]{1,0:T(1,128)S(1)}) custom-call(f32[8,32,256]{2,1,0:T(8,128)S(1)} %bitcast.11, f32[8,256]{1,0:T(8,128)S(1)} %bitcast.16, bf16[8,9,256,256]{3,2,1,0:T(8,128)(2,1)} %bitcast.19, bf16[8,64,256]{2,1,0:T(8,128)(2,1)S(1)} %bitcast.12, s32[1,64]{1,0:T(1,128)S(1)} %bitcast.17, ...), custom_call_target="tpu_custom_call" | custom-call | tf_op jit(solution)/shard_map/pallas_call | solution.py:264
  68.7 0.5 slice_bitcast_fusion
  69.2 0.7 copy.12
  69.9 0.7 copy.13
Async XLA Ops:
  0.6 1.0 %copy-start = (f32[1,1,8,32,256]{4,3,2,1,0:T(8,128)S(1)}, f32[1,1,8,32,256]{4,3,2,1,0:T(8,128)}, u32[]{:S(2)}) copy-start(f32[1,1,8,32,256]{4,3,2,1,0:T(8,128)} %param.7) | copy-start | bytes 786436
  1.6 0.9 %copy-start.1 = (bf16[1,1,8,64,256]{4,3,2,1,0:T(8,128)(2,1)S(1)}, bf16[1,1,8,64,256]{4,3,2,1,0:T(8,128)(2,1)}, u32[]{:S(2)}) copy-start(bf16[1,1,8,64,256]{4,3,2,1,0:T(8,128)(2,1)} %param.10) | copy-start | bytes 786436
  2.5 0.9 %copy-start.2 = (bf16[1,1,7,64,64]{4,3,2,1,0:T(8,128)(2,1)S(1)}, bf16[1,1,7,64,64]{4,3,2,1,0:T(8,128)(2,1)}, u32[]{:S(2)}) copy-start(bf16[1,1,7,64,64]{4,3,2,1,0:T(8,128)(2,1)} %param.13) | copy-start | bytes 172036
  3.4 0.7 copy-start.3
  4.1 0.7 copy-start.4
  4.8 0.7 copy-start.5

commit v2 on v1

--- a/solution.py
+++ b/solution.py
@@ -24,7 +24,7 @@
 
 
 def each(count, body):
-    if count <= 16:
+    if count <= 32:
         for i in range(count):
             body(i)
     else:
@@ -33,16 +33,27 @@
 
 def kernel(
     n_row, n_blk, tracers,
-    right_ref, noise_ref, blocks_hbm, basis_ref, index_ref, far_ref, coupling_ref,
+    right_hbm, noise_hbm, blocks_hbm, basis_hbm, index_ref, far_ref, coupling_hbm,
     solution_ref, residual_ref, quadratic_ref,
-    blocks, mixed, extended, direction, applied, skeletons, row_sums, blk_sums,
-    load_sem, halo_send, halo_recv, skel_send, skel_recv, row_send, row_recv, blk_send, blk_recv,
+    right_ref, noise_ref, coupling_ref, blocks, mixed, extended, direction, applied, skeletons, sums_all,
+    first_sem, load_sem, halo_send, halo_recv, skel_send, skel_recv, sum_send, sum_recv,
 ):
     leaves, columns, width = right_ref.shape
-    rank = basis_ref.shape[1]
+    rank = basis_hbm.shape[1]
     far_count = coupling_ref.shape[0]
     my_row, my_blk = lax.axis_index("row"), lax.axis_index("blk")
 
+    firsts = [
+        pltpu.make_async_copy(source, target, first_sem.at[i])
+        for i, (source, target) in enumerate((
+            (right_hbm, right_ref),
+            (basis_hbm, mixed.at[:, pl.ds(0, rank)]),
+            (noise_hbm, noise_ref),
+            (coupling_hbm, coupling_ref),
+        ))
+    ]
+    for first_load in firsts:
+        first_load.start()
     loads = [
         pltpu.make_async_copy(blocks_hbm.at[l], blocks.at[l], load_sem.at[l]) for l in range(leaves)
     ]
@@ -60,11 +71,8 @@
     def greet(row, blk):
         pl.semaphore_signal(barrier, inc=1, device_id={"row": row, "blk": blk}, device_id_type=MESH)
 
-    for o in range(1, n_row):
-        greet(row_at(o), my_blk)
-    each(n_blk - 1, lambda i: greet(my_row, blk_at(i + 1)))
-    for dr, dc in SHIFTS[4:]:
-        greet(row_at(dr), blk_at(dc))
+    devices = n_row * n_blk
+    each(devices - 1, lambda i: greet(row_at((i + 1) // n_blk), blk_at((i + 1) % n_blk)))
 
     sublane = lax.broadcasted_iota(jnp.int32, (rank, rank), 0)
     lane = lax.broadcasted_iota(jnp.int32, (rank, rank), 1)
@@ -73,21 +81,22 @@
     point = lax.broadcasted_iota(jnp.int32, (rank, width), 1).astype(jnp.float32)
     for l in range(leaves):
         picks = jnp.where(point + float(width * l) == as_column, 1.0, 0.0).astype(jnp.bfloat16)
-        mixed[l, :rank] = basis_ref[l]
         mixed[l, rank : 2 * rank] = picks
         mixed[l, 2 * rank :] = picks
+    quadratic_ref[...] = jnp.zeros_like(quadratic_ref)
+    for first_load in firsts:
+        first_load.wait()
+    for l in range(leaves):
         value = right_ref[l]
         direction[l] = value
         residual_ref[l] = value
         solution_ref[l] = jnp.zeros_like(value)
-    quadratic_ref[...] = jnp.zeros_like(quadratic_ref)
-
-    pl.semaphore_wait(barrier, (n_row - 1) + (n_blk - 1) + 4)
+
+    pl.semaphore_wait(barrier, devices - 1)
 
     ones = jnp.ones((8, 128), jnp.float32)
-    head = lax.broadcasted_iota(jnp.int32, (8, columns), 0)
-    spread_row = lax.broadcasted_iota(jnp.int32, (columns, 128), 0)
-    spread_lane = lax.broadcasted_iota(jnp.int32, (columns, 128), 1)
+    spread_row = lax.broadcasted_iota(jnp.int32, (columns, columns), 0)
+    spread_lane = lax.broadcasted_iota(jnp.int32, (columns, columns), 1)
 
     def halo(k, n):
         dr, dc = SHIFTS[n]
@@ -102,13 +111,15 @@
             device_id_type=MESH,
         )
 
-    def row_copy(k, o):
+    me = my_row * n_blk + my_blk
+
+    def sum_copy(k, i):
         return pltpu.make_async_remote_copy(
-            src_ref=row_sums.at[k, my_row],
-            dst_ref=row_sums.at[k, my_row],
-            send_sem=row_send.at[k, o - 1],
-            recv_sem=row_recv.at[k, o - 1],
-            device_id={"row": row_at(o), "blk": my_blk},
+            src_ref=sums_all.at[k, me],
+            dst_ref=sums_all.at[k, me],
+            send_sem=sum_send.at[k],
+            recv_sem=sum_recv.at[k],
+            device_id={"row": row_at(i // n_blk), "blk": blk_at(i % n_blk)},
             device_id_type=MESH,
         )
 
@@ -122,8 +133,8 @@
             device_id_type=MESH,
         )
 
-    def blk_wait(buffer, sem, k):
-        every = buffer.at[k, pl.ds(0, n_blk - 1)]
+    def all_wait(buffer, sem, k, count):
+        every = buffer.at[k, pl.ds(0, count - 1)]
         pltpu.make_async_copy(every, every, sem.at[k]).wait()
 
     def slots(l):
@@ -165,7 +176,7 @@
                     )
             applied[l] = total
 
-        blk_wait(skeletons, skel_recv, k)
+        all_wait(skeletons, skel_recv, k, n_blk)
         far = jnp.zeros((columns, rank), jnp.float32)
         for j in range(far_count):
             far = far + jnp.dot(
@@ -192,41 +203,26 @@
                 for h in range(width // 128):
                     sums[q] = sums[q] + product[:, 128 * h : 128 * (h + 1)]
 
-        part = jnp.zeros((8, columns), jnp.float32)
-        for q in range(5):
-            line = lax.dot_general(
-                ones, sums[q], (((1,), (1,)), ((), ())),
-                precision=HIGHEST, preferred_element_type=jnp.float32,
-            )
-            part = jnp.where(head == q, line, part)
-        row_sums[k, my_row] = jnp.concatenate(
-            [part, jnp.zeros((8, 128 - columns), jnp.float32)], axis=1
-        )
-        for o in range(1, n_row):
-            row_copy(k, o).start()
-        for o in range(1, n_row):
-            row_copy(k, o).wait_recv()
-        in_row = row_sums[k, 0]
-        for i in range(1, n_row):
-            in_row = in_row + row_sums[k, i]
-        blk_sums[k, my_blk] = in_row
-        each(n_blk - 1, lambda i: blk_copy(blk_sums, blk_send, blk_recv, k, i + 1).start())
-        blk_wait(blk_sums, blk_recv, k)
-        if n_blk <= 16:
-            whole = blk_sums[k, 0]
-            for i in range(1, n_blk):
-                whole = whole + blk_sums[k, i]
-        else:
-            whole = jnp.sum(blk_sums[k], axis=0)
-
-        curve, cross, square, data, norm = (whole[q : q + 1] for q in range(5))
+        rest = jnp.zeros((256 - 5 * columns, 128), jnp.float32)
+        lines = lax.dot_general(
+            ones, jnp.concatenate(sums + [rest], axis=0), (((1,), (1,)), ((), ())),
+            precision=HIGHEST, preferred_element_type=jnp.float32,
+        )
+        sums_all[k, me] = lines[:1]
+        each(devices - 1, lambda i: sum_copy(k, i + 1).start())
+        all_wait(sums_all, sum_recv, k, devices)
+        whole = jnp.sum(sums_all[k], axis=0)
+
+        curve, cross, square, data, norm = (
+            whole[:, q * columns : (q + 1) * columns] for q in range(5)
+        )
         step = norm / curve
         norm_next = jnp.maximum(norm - 2.0 * step * cross + step * step * square, 0.0)
         turn = norm_next / norm
         quadratic_ref[...] = quadratic_ref[...] + step * data * (1.0 / tracers)
 
         def per_column(line):
-            wide = jnp.broadcast_to(line, (columns, 128))
+            wide = jnp.broadcast_to(line, (columns, columns))
             kept = jnp.where(spread_row == spread_lane, wide, 0.0)
             return jnp.sum(kept, axis=1, keepdims=True)
 
@@ -238,18 +234,18 @@
             residual_ref[l] = r
             direction[l] = r + turn_c * d
 
-        for n in range(8):
-            halo(k, n).wait_send()
-        for o in range(1, n_row):
-            row_copy(k, o).wait_send()
-        blk_wait(skeletons, skel_send, k)
-        blk_wait(blk_sums, blk_send, k)
-
     iteration(0, True)
 
     @pl.loop(1, ITERS)
     def _(k):
         iteration(k, False)
+
+    @pl.loop(0, ITERS)
+    def _(k):
+        for n in range(8):
+            halo(k, n).wait_send()
+        all_wait(skeletons, skel_send, k, n_blk)
+        all_wait(sums_all, sum_send, k, devices)
 
 
 def local(
@@ -260,28 +256,29 @@
     rank = skeleton_basis.shape[3]
     field = jax.ShapeDtypeStruct((leaves, columns, width), jnp.float32)
     vmem = pl.BlockSpec(memory_space=pltpu.VMEM)
+    hbm = pl.BlockSpec(memory_space=pltpu.HBM)
     dma = pltpu.SemaphoreType.DMA
     solution_out, residual_out, quadratic = pl.pallas_call(
         functools.partial(kernel, n_row, n_blk, n_row * n_blk * leaves * width),
-        out_shape=(field, field, jax.ShapeDtypeStruct((1, 128), jnp.float32)),
+        out_shape=(field, field, jax.ShapeDtypeStruct((1, columns), jnp.float32)),
         in_specs=[
-            vmem, vmem, pl.BlockSpec(memory_space=pl.ANY), vmem, vmem,
-            pl.BlockSpec(memory_space=pltpu.SMEM), vmem,
+            hbm, hbm, hbm, hbm, vmem, pl.BlockSpec(memory_space=pltpu.SMEM), hbm,
         ],
         out_specs=(vmem, vmem, vmem),
         scratch_shapes=[
+            pltpu.VMEM((leaves, columns, width), jnp.float32),
+            pltpu.VMEM(noise_level.shape[2:], jnp.float32),
+            pltpu.VMEM(couplings.shape[2:], jnp.bfloat16),
             pltpu.VMEM(near_blocks.shape[2:], jnp.bfloat16),
             pltpu.VMEM((leaves, 3 * rank, width), jnp.bfloat16),
             pltpu.VMEM((ITERS, LEAF_ROWS + 2, LEAF_COLS + 2, columns, width), jnp.bfloat16),
             pltpu.VMEM((leaves, columns, width), jnp.float32),
             pltpu.VMEM((leaves, columns, width), jnp.float32),
             pltpu.VMEM((ITERS, n_blk, columns, rank), jnp.bfloat16),
-            pltpu.VMEM((ITERS, n_row, 8, 128), jnp.float32),
-            pltpu.VMEM((ITERS, n_blk, 8, 128), jnp.float32),
-            dma((leaves,)),
+            pltpu.VMEM((ITERS, n_row * n_blk, 1, 256), jnp.float32),
+            dma((4,)), dma((leaves,)),
             dma((ITERS, 8)), dma((ITERS, 8)),
             dma((ITERS,)), dma((ITERS,)),
-            dma((ITERS, n_row - 1)), dma((ITERS, n_row - 1)),
             dma((ITERS,)), dma((ITERS,)),
         ],
         compiler_params=pltpu.CompilerParams(
@@ -291,7 +288,7 @@
         right_side[0, 0], noise_level[0, 0], near_blocks[0, 0], skeleton_basis[0, 0],
         skeleton_index[0], far_list[0], couplings[0, 0],
     )
-    return solution_out[None, None], residual_out[None, None], quadratic[0, :columns]
+    return solution_out[None, None], residual_out[None, None], quadratic[0]
 
 
 def solution(mesh):

time: 70.9 us -> 64.9 us (0.915)
  Pallas kernels: 63.2 us -> 57.3 us
    pallas_call x1, Pallas kernels: 63.2 us -> 57.3 us  [local(): pl.pallas_call(functools.partial(kernel, n_row, n_blk, n_row * n_blk * le...]
    unnamed x14 -> x15, local copies, waits for them, and re-layouts: 6.2 us -> 6.71 us
where the time goes in v2:
time: 64.9 us; the launch traced here: 64.6 us
  Pallas kernels  57.3 us (88%)
  local copies, waits for them, and re-layouts  6.71 us (10%)
  between operations  0.66 us (1%)
    pallas_call x1, Pallas kernels, local(): pl.pallas_call(functools.partial(kernel, n_row, n_blk, n_row * n_blk * le...  57.3 us
    unnamed x15, local copies, waits for them, and re-layouts  6.71 us

profile of v2, /device:TPU:0, one launch (start us, length us, event | category | flops | bytes accessed | tf_op | source)
XLA Modules:
  0.0 64.6 jit_solution(4015403770315383557)
XLA Ops:
  0.6 0.0 copy-start
  0.6 0.9 %copy-done = f32[1,1,8,32,256]{4,3,2,1,0:T(8,128)S(1)} copy-done((f32[1,1,8,32,256]{4,3,2,1,0:T(8,128)S(1)}, f32[1,1,8,32,256]{4,3,2,1,0:T(8,128)}, u32[]{:S(2)}) %copy-start) | copy-done | bytes 262168
  1.6 0.0 copy-start.1
  1.6 0.9 %copy-done.1 = bf16[1,1,8,64,256]{4,3,2,1,0:T(8,128)(2,1)S(1)} copy-done((bf16[1,1,8,64,256]{4,3,2,1,0:T(8,128)(2,1)S(1)}, bf16[1,1,8,64,256]{4,3,2,1,0:T(8,128)(2,1)}, u32[]{:S(2)}) %copy-start.1) | copy-done | bytes 262168
  2.5 0.0 copy-start.2
  2.5 0.9 %copy-done.2 = bf16[1,1,7,64,64]{4,3,2,1,0:T(8,128)(2,1)S(1)} copy-done((bf16[1,1,7,64,64]{4,3,2,1,0:T(8,128)(2,1)S(1)}, bf16[1,1,7,64,64]{4,3,2,1,0:T(8,128)(2,1)}, u32[]{:S(2)}) %copy-start.2) | copy-done | bytes 57368
  3.4 0.0 copy-start.3
  3.4 0.7 %copy-done.3 = f32[1,1,8,256]{3,2,1,0:T(8,128)S(1)} copy-done((f32[1,1,8,256]{3,2,1,0:T(8,128)S(1)}, f32[1,1,8,256]{3,2,1,0:T(8,128)}, u32[]{:S(2)}) %copy-start.3) | copy-done | bytes 8216
  4.1 0.0 copy-start.4
  4.1 0.7 %copy-done.4 = s32[1,1,64]{2,1,0:T(1,128)S(1)} copy-done((s32[1,1,64]{2,1,0:T(1,128)S(1)}, s32[1,1,64]{2,1,0:T(1,128)}, u32[]{:S(2)}) %copy-start.4) | copy-done | bytes 280
  4.8 0.0 copy-start.5
  4.8 0.7 %copy-done.5 = s32[1,1,7]{2,1,0:T(1,128)S(1)} copy-done((s32[1,1,7]{2,1,0:T(1,128)S(1)}, s32[1,1,7]{2,1,0:T(1,128)}, u32[]{:S(2)}) %copy-start.5) | copy-done | bytes 52
  5.4 57.3 %shard_map.94 = (f32[8,32,256]{2,1,0:T(8,128)S(1)}, f32[8,32,256]{2,1,0:T(8,128)S(1)}, f32[1,32]{1,0:T(1,128)S(1)}) custom-call(f32[8,32,256]{2,1,0:T(8,128)S(1)} %bitcast.10, f32[8,256]{1,0:T(8,128)S(1)} %bitcast.15, bf16[8,9,256,256]{3,2,1,0:T(8,128)(2,1)} %bitcast.19, bf16[8,64,256]{2,1,0:T(8,128)(2,1)S(1)} %bitcast.11, s32[1,64]{1,0:T(1,128)S(1)} %bitcast.16, ...), custom_call_target="tpu_custom_call" | custom-call | tf_op jit(solution)/shard_map/pallas_call | solution.py:261
  62.7 0.7 %copy.13 = f32[1,1,8,32,256]{4,3,2,1,0:T(8,128)} copy(f32[1,1,8,32,256]{4,3,2,1,0:T(8,128)S(1)} %bitcast.13) | data formatting | bytes 524288
  63.4 0.7 %copy.14 = f32[1,1,8,32,256]{4,3,2,1,0:T(8,128)} copy(f32[1,1,8,32,256]{4,3,2,1,0:T(8,128)S(1)} %bitcast.12) | data formatting | bytes 524288
  64.1 0.5 copy.15
Async XLA Ops:
  0.6 1.0 %copy-start = (f32[1,1,8,32,256]{4,3,2,1,0:T(8,128)S(1)}, f32[1,1,8,32,256]{4,3,2,1,0:T(8,128)}, u32[]{:S(2)}) copy-start(f32[1,1,8,32,256]{4,3,2,1,0:T(8,128)} %param.7) | copy-start | bytes 786436
  1.6 0.9 %copy-start.1 = (bf16[1,1,8,64,256]{4,3,2,1,0:T(8,128)(2,1)S(1)}, bf16[1,1,8,64,256]{4,3,2,1,0:T(8,128)(2,1)}, u32[]{:S(2)}) copy-start(bf16[1,1,8,64,256]{4,3,2,1,0:T(8,128)(2,1)} %param.10) | copy-start | bytes 786436
  2.5 0.9 %copy-start.2 = (bf16[1,1,7,64,64]{4,3,2,1,0:T(8,128)(2,1)S(1)}, bf16[1,1,7,64,64]{4,3,2,1,0:T(8,128)(2,1)}, u32[]{:S(2)}) copy-start(bf16[1,1,7,64,64]{4,3,2,1,0:T(8,128)(2,1)} %param.13) | copy-start | bytes 172036
  3.4 0.7 %copy-start.3 = (f32[1,1,8,256]{3,2,1,0:T(8,128)S(1)}, f32[1,1,8,256]{3,2,1,0:T(8,128)}, u32[]{:S(2)}) copy-start(f32[1,1,8,256]{3,2,1,0:T(8,128)} %param.8) | copy-start | bytes 24580
  4.1 0.7 %copy-start.4 = (s32[1,1,64]{2,1,0:T(1,128)S(1)}, s32[1,1,64]{2,1,0:T(1,128)}, u32[]{:S(2)}) copy-start(s32[1,1,64]{2,1,0:T(1,128)} %param.11) | copy-start | bytes 772
  4.8 0.7 %copy-start.5 = (s32[1,1,7]{2,1,0:T(1,128)S(1)}, s32[1,1,7]{2,1,0:T(1,128)}, u32[]{:S(2)}) copy-start(s32[1,1,7]{2,1,0:T(1,128)} %param.12) | copy-start | bytes 88

commit v3 on v2

--- a/solution.py
+++ b/solution.py
@@ -209,7 +209,7 @@
             precision=HIGHEST, preferred_element_type=jnp.float32,
         )
         sums_all[k, me] = lines[:1]
-        each(devices - 1, lambda i: sum_copy(k, i + 1).start())
+        each(devices - 1, lambda i: sum_copy(k, devices - 1 - i).start())
         all_wait(sums_all, sum_recv, k, devices)
         whole = jnp.sum(sums_all[k], axis=0)
 
@@ -282,7 +282,7 @@
             dma((ITERS,)), dma((ITERS,)),
         ],
         compiler_params=pltpu.CompilerParams(
-            collective_id=0, has_side_effects=True, vmem_limit_bytes=48 * 1024 * 1024
+            collective_id=0, has_side_effects=True, vmem_limit_bytes=63 * 1024 * 1024
         ),
     )(
         right_side[0, 0], noise_level[0, 0], near_blocks[0, 0], skeleton_basis[0, 0],

time: 64.9 us -> 62.3 us (0.960)
  local copies, waits for them, and re-layouts: 6.71 us -> 4.45 us
    unnamed x15 -> x3, local copies, waits for them, and re-layouts: 6.71 us -> 4.45 us
where the time goes in v3:
time: 62.3 us; the launch traced here: 62.1 us
  Pallas kernels  57 us (91%)
  local copies, waits for them, and re-layouts  4.45 us (7%)
  between operations  0.64 us (1%)
    pallas_call x1, Pallas kernels, local(): pl.pallas_call(functools.partial(kernel, n_row, n_blk, n_row * n_blk * le...  57 us
    unnamed x3, local copies, waits for them, and re-layouts  4.45 us

profile of v3, /device:TPU:0, one launch (start us, length us, event | category | flops | bytes accessed | tf_op | source)
XLA Modules:
  0.0 62.1 jit_solution(14046466787474795896)
XLA Ops:
  0.6 57.0 %shard_map.94 = (f32[8,32,256]{2,1,0:T(8,128)}, f32[8,32,256]{2,1,0:T(8,128)}, f32[1,32]{1,0:T(1,128)}) custom-call(f32[8,32,256]{2,1,0:T(8,128)} %bitcast.11, f32[8,256]{1,0:T(8,128)} %bitcast.16, bf16[8,9,256,256]{3,2,1,0:T(8,128)(2,1)} %bitcast.10, bf16[8,64,256]{2,1,0:T(8,128)(2,1)} %bitcast.12, s32[1,64]{1,0:T(1,128)} %bitcast.17, s32[1,7]{1,0:T(1,128)} %bitcast.18, ...), custom_call_target="tpu_custom_call" | custom-call | tf_op jit(solution)/shard_map/pallas_call | solution.py:261
  57.7 1.7 %copy.13 = f32[1,1,8,32,256]{4,3,2,1,0:T(8,128)} copy(f32[1,1,8,32,256]{4,3,2,1,0:T(8,128)} %bitcast.14) | data formatting | bytes 524288
  59.3 1.7 %copy.14 = f32[1,1,8,32,256]{4,3,2,1,0:T(8,128)} copy(f32[1,1,8,32,256]{4,3,2,1,0:T(8,128)} %bitcast.13) | data formatting | bytes 524288
  61.0 1.1 %copy.15 = f32[32]{0:T(128)} copy(f32[32]{0:T(128)} %bitcast.19) | data formatting | bytes 256

commit v4 on v3

--- a/solution.py
+++ b/solution.py
@@ -176,6 +176,16 @@
                     )
             applied[l] = total
 
+        sums = [jnp.zeros((columns, 128), jnp.float32) for _ in range(5)]
+
+        def add(q, product):
+            for h in range(width // 128):
+                sums[q] = sums[q] + product[:, 128 * h : 128 * (h + 1)]
+
+        for l in range(leaves):
+            add(3, right_ref[l] * direction[l])
+            add(4, residual_ref[l] * residual_ref[l])
+
         all_wait(skeletons, skel_recv, k, n_blk)
         far = jnp.zeros((columns, rank), jnp.float32)
         for j in range(far_count):
@@ -189,7 +199,6 @@
         for n in range(8):
             halo(k, n).wait_recv()
 
-        sums = [jnp.zeros((columns, 128), jnp.float32) for _ in range(5)]
         for l in range(leaves):
             total = applied[l] + jnp.dot(far_all, mixed[l], preferred_element_type=jnp.float32)
             for s, row, col in slots(l):
@@ -199,9 +208,9 @@
                     )
             applied[l] = total
             d, r = direction[l], residual_ref[l]
-            for q, product in enumerate((d * total, r * total, total * total, right_ref[l] * d, r * r)):
-                for h in range(width // 128):
-                    sums[q] = sums[q] + product[:, 128 * h : 128 * (h + 1)]
+            add(0, d * total)
+            add(1, r * total)
+            add(2, total * total)
 
         rest = jnp.zeros((256 - 5 * columns, 128), jnp.float32)
         lines = lax.dot_general(

time: 62.3 us -> 62.3 us (level)
  no operation moved by 1% of the time
where the time goes in v4:
time: 62.3 us; the launch traced here: 62.1 us
  Pallas kernels  57 us (91%)
  local copies, waits for them, and re-layouts  4.45 us (7%)
  between operations  0.64 us (1%)
    pallas_call x1, Pallas kernels, local(): pl.pallas_call(functools.partial(kernel, n_row, n_blk, n_row * n_blk * le...  57 us
    unnamed x3, local copies, waits for them, and re-layouts  4.45 us

profile of v4, /device:TPU:0, one launch (start us, length us, event | category | flops | bytes accessed | tf_op | source)
XLA Modules:
  0.0 62.1 jit_solution(3504497996330915872)
XLA Ops:
  0.6 57.0 %shard_map.94 = (f32[8,32,256]{2,1,0:T(8,128)}, f32[8,32,256]{2,1,0:T(8,128)}, f32[1,32]{1,0:T(1,128)}) custom-call(f32[8,32,256]{2,1,0:T(8,128)} %bitcast.11, f32[8,256]{1,0:T(8,128)} %bitcast.16, bf16[8,9,256,256]{3,2,1,0:T(8,128)(2,1)} %bitcast.10, bf16[8,64,256]{2,1,0:T(8,128)(2,1)} %bitcast.12, s32[1,64]{1,0:T(1,128)} %bitcast.17, s32[1,7]{1,0:T(1,128)} %bitcast.18, ...), custom_call_target="tpu_custom_call" | custom-call | tf_op jit(solution)/shard_map/pallas_call | solution.py:270
  57.7 1.7 %copy.13 = f32[1,1,8,32,256]{4,3,2,1,0:T(8,128)} copy(f32[1,1,8,32,256]{4,3,2,1,0:T(8,128)} %bitcast.14) | data formatting | bytes 524288
  59.4 1.7 %copy.14 = f32[1,1,8,32,256]{4,3,2,1,0:T(8,128)} copy(f32[1,1,8,32,256]{4,3,2,1,0:T(8,128)} %bitcast.13) | data formatting | bytes 524288
  61.0 1.1 %copy.15 = f32[32]{0:T(128)} copy(f32[32]{0:T(128)} %bitcast.19) | data formatting | bytes 256
